TPU v7x, 32 devices: a whole 2x2x4 slice. The times are simulated.
32 devices in a mesh: dec: 2 (over x), ada: 16 (over z, y, core).
Axes of the slice: x: 2, y: 2, z: 4, core: 2. Of those that a mesh axis runs over, the one named last changes fastest.
Arguments:
- inputs: bfloat16 [4, 64, 8192], P(None, ('dec', 'ada')), may hold values from -6 to 6
- query_weight: bfloat16 [8192, 8192], P(None, 'ada'), may hold values from -0.0625 to 0.0625
- adapter_down: bfloat16 [32, 8192, 64], P(('dec', 'ada')), may hold values from -0.0625 to 0.0625
- adapter_up: bfloat16 [32, 64, 8192], P(('dec', 'ada')), may hold values from -0.75 to 0.75
- adapter_ids: int32 [64, 1], P(('dec', 'ada')), may hold values from 0 to 15; in each aligned block of 32 rows (0 to 31, 32 to 63, ...) at most 4 rows name the same one
- new_cache: bfloat16 [4, 64, 2, 1024], P(None, ('dec', 'ada')), may hold values from -9 to 9
- cache_pool: bfloat16 [256, 2, 16, 1024], P(('dec', 'ada')), may hold values from -400 to 400
- page_table: int32 [64, 4], P(('dec', 'ada')), may hold values from 0 to 15, as said below
- lengths: int32 [64], P(('dec', 'ada')), may hold values from 1 to 64, as said below
Outputs:
- attended: bfloat16 [4, 64, 8192], P(None, ('dec', 'ada'))
Inputs may be any that keep to these rules, and one draw needn't show every extreme that they name: `adapter_ids`: in each aligned block of 32 rows (one decode group) no id is named by more than 4 rows, a bound that some block reaches. `page_table`: entries j >= ceil(lengths[r] / 16) are unused. Among rows with the same (r % 32) // 2, the live entries are all different. `lengths`: among rows with the same (r % 32) // 2, one reaches 64.
All inputs are finite; a program needn't handle non-finite values.
Results may differ from a plain program's by a relative error of at most 0.007.
The roundings to bfloat16 on the way count: a program that leaves them out, or rounds other values in their place, can miss the bound.
Values may be sent and summed in bfloat16 or wider, within the bound.
A program may use at most 64 MiB of HBM per device.

v0:
```python
import math
import jax
import jax.numpy as jnp
from jax import lax
from jax.sharding import PartitionSpec as P

HEADS = 64
KVH = 8
HD = 128
CAP = 4
NEGATIVE = -1e30
HIGH = lax.Precision.HIGHEST


def cache_part(query, keys, values, live):
    scale = 1.0 / math.sqrt(query.shape[-1])
    scores = (
        jnp.einsum("trkgd,rpkd->trkgp", query, keys, preferred_element_type=jnp.float32) * scale
    )
    mask = live[None, :, None, None, :]
    scores = jnp.where(mask, scores, NEGATIVE)
    top = jnp.max(scores, axis=-1)
    weights = jnp.where(mask, jnp.exp(scores - top[..., None]), 0.0)
    numerator = jnp.einsum("trkgp,rpkd->trkgd", weights, values.astype(jnp.float32), precision=HIGH)
    return (numerator, top, jnp.sum(weights, axis=-1))


def fresh_part(query, new_entries):
    steps, rows, kv_heads, group, head_dim = query.shape
    scale = 1.0 / math.sqrt(head_dim)
    keys = new_entries[:, :, 0].reshape(new_entries.shape[0], rows, kv_heads, head_dim)
    values = new_entries[:, :, 1].reshape(new_entries.shape[0], rows, kv_heads, head_dim)
    scores = (
        jnp.einsum("trkgd,urkd->trkgu", query, keys, preferred_element_type=jnp.float32) * scale
    )
    allowed = (jnp.arange(new_entries.shape[0])[None, :] <= jnp.arange(steps)[:, None])[
        :, None, None, None, :
    ]
    scores = jnp.where(allowed, scores, NEGATIVE)
    top = jnp.max(scores, axis=-1)
    weights = jnp.where(allowed, jnp.exp(scores - top[..., None]), 0.0)
    numerator = jnp.einsum("trkgu,urkd->trkgd", weights, values.astype(jnp.float32), precision=HIGH)
    return (numerator, top, jnp.sum(weights, axis=-1))


def body(
    inputs,
    query_weight,
    adapter_down,
    adapter_up,
    adapter_ids,
    new_cache,
    cache_pool,
    page_table,
    lengths,
):
    steps, row_local, width = inputs.shape
    adapter_total_count = lax.axis_size("ada")
    dec_count = lax.axis_size("dec")
    head_cols = query_weight.shape[1]
    held_adapters = adapter_down.shape[0]
    adapter_rank = adapter_down.shape[2]
    group = row_local * adapter_total_count
    capacity = CAP
    slots = held_adapters * capacity
    whole_inputs, group_ids = (
        lax.all_gather(inputs, "ada", axis=1, tiled=True),
        lax.all_gather(adapter_ids, "ada", axis=0, tiled=True),
    )
    base_output = jnp.dot(
        whole_inputs.reshape(steps * group, width), query_weight, preferred_element_type=jnp.float32
    )
    base_output = base_output.reshape(steps, group, head_cols)
    row_adapter = group_ids[:, 0]
    order = jnp.arange(group)
    earlier = (row_adapter[:, None] == row_adapter[None, :]) & (order[None, :] < order[:, None])
    earlier_count = jnp.sum(earlier.astype(jnp.int32), axis=1)
    slot_of_row = (
        row_adapter // held_adapters * slots
        + row_adapter % held_adapters * capacity
        + earlier_count
    )
    local_slot = slot_of_row - lax.axis_index("ada") * slots
    pick = (local_slot[None, :] == jnp.arange(slots)[:, None]).astype(jnp.bfloat16)
    chosen = jnp.einsum(
        "sg,tgd->tsd", pick, whole_inputs, preferred_element_type=jnp.float32
    ).astype(jnp.bfloat16)
    chosen = chosen.reshape(steps, held_adapters, capacity, width)
    shrink = jnp.einsum(
        "tjcd,jdr->tjcr", chosen, adapter_down, preferred_element_type=jnp.float32
    ).astype(jnp.bfloat16)
    columns = lax.all_to_all(adapter_up, "ada", split_axis=2, concat_axis=0, tiled=True)
    every_shrink = lax.all_gather(
        shrink.reshape(steps, slots, adapter_rank), "ada", axis=1, tiled=True
    )
    every_shrink = every_shrink.reshape(
        steps, adapter_total_count * held_adapters, capacity, adapter_rank
    )
    received_rows = jnp.einsum(
        "tacr,arh->tach", every_shrink, columns, preferred_element_type=jnp.float32
    ).astype(jnp.bfloat16)
    received_rows = received_rows.reshape(steps, adapter_total_count * slots, head_cols)
    slot_position = (
        slot_of_row[:, None] == jnp.arange(adapter_total_count * slots)[None, :]
    ).astype(jnp.bfloat16)
    low_rank_update = jnp.einsum(
        "mr,urx->umx", slot_position, received_rows, preferred_element_type=jnp.float32
    )
    query_columns = (base_output + low_rank_update).astype(jnp.bfloat16)
    query_local = lax.all_to_all(query_columns, "ada", split_axis=1, concat_axis=2, tiled=True)
    group_heads = HEADS // KVH
    query = query_local.reshape(steps, row_local, KVH, group_heads, HD)
    fresh = fresh_part(query, new_cache)
    pool_local = cache_pool.shape[0]
    page_length = cache_pool.shape[2]
    table_width = page_table.shape[1]
    position = jnp.arange(table_width * page_length)
    every_query, every_table, every_length = (
        lax.all_gather(query_local, "dec", axis=1, tiled=True),
        lax.all_gather(page_table, "dec", axis=0, tiled=True),
        lax.all_gather(lengths, "dec", axis=0, tiled=True),
    )
    column_rows = dec_count * row_local
    asked = every_query.reshape(steps, column_rows, KVH, group_heads, HD)
    local = every_table // pool_local == lax.axis_index("dec")
    pages = cache_pool[every_table % pool_local]
    keys = pages[:, :, 0].reshape(column_rows, table_width * page_length, KVH, HD)
    values = pages[:, :, 1].reshape(column_rows, table_width * page_length, KVH, HD)
    live = (position[None, :] < every_length[:, None]) & jnp.repeat(local, page_length, axis=1)
    partial_numerator, part_top, part_total = cache_part(asked, keys, values, live)
    partial_numerator = partial_numerator.reshape(steps, dec_count, row_local, KVH, group_heads, HD)
    part_top = part_top.reshape(steps, dec_count, row_local, KVH, group_heads)
    part_total = part_total.reshape(steps, dec_count, row_local, KVH, group_heads)
    back_numerator, back_top, back_total = (
        lax.all_to_all(partial_numerator, "dec", split_axis=1, concat_axis=1, tiled=True),
        lax.all_to_all(part_top, "dec", split_axis=1, concat_axis=1, tiled=True),
        lax.all_to_all(part_total, "dec", split_axis=1, concat_axis=1, tiled=True),
    )
    top = jnp.maximum(jnp.max(back_top, axis=1), fresh[1])
    factor = jnp.exp(back_top - top[:, None])
    numerator = (
        jnp.sum(back_numerator * factor[..., None], axis=1)
        + fresh[0] * jnp.exp(fresh[1] - top)[..., None]
    )
    total = jnp.sum(back_total * factor, axis=1) + fresh[2] * jnp.exp(fresh[1] - top)
    attended = (numerator / total[..., None]).astype(jnp.bfloat16)
    return attended.reshape(steps, row_local, width)


def solution(mesh):
    in_specs = (
        P(None, ("dec", "ada"), None),
        P(None, "ada"),
        P(("dec", "ada"), None, None),
        P(("dec", "ada"), None, None),
        P(("dec", "ada"), None),
        P(None, ("dec", "ada"), None, None),
        P(("dec", "ada"), None, None, None),
        P(("dec", "ada"), None),
        P(("dec", "ada")),
    )
    out_specs = P(None, ("dec", "ada"), None)
    return jax.shard_map(body, mesh=mesh, in_specs=in_specs, out_specs=out_specs, check_vma=False)
```

profile of v0, /device:TPU:0, one launch (start us, length us, event | category | flops | bytes accessed | tf_op | source)
XLA Modules:
  0.0 197.2 jit_solution(16430546696477317186)
XLA Ops:
  6.5 1.8 copy.73
  8.3 9.2 %copy.78 = bf16[1,64,8192]{1,0,2:T(2,128)(2,1)} copy(bf16[1,64,8192]{2,1,0:T(8,128)(2,1)} %param.12) | data formatting | bytes 2097152 | tf_op args[3]
  17.5 0.5 broadcast.160
  18.0 45.2 %reduce.4 = bf16[8192,64]{1,0:T(8,128)(2,1)S(1)} reduce(bf16[8192,1,64]{2,1,0:T(2,128)(2,1)} %bitcast.122, bf16[]{:T(256)} %broadcast.160), dimensions={1}, to_apply=%bitcast.103.reduce_sub_computation | reduce | bytes 2097154
  63.2 2.3 %reshape.164 = bf16[16,2,16384]{2,1,0:T(2,128)(2,1)} reshape(bf16[8192,64]{1,0:T(8,128)(2,1)S(1)} %reduce.4) | data formatting | bytes 2097152
  65.5 7.4 %all-to-all-start = ((bf16[16,2,16384]{2,1,0:T(2,128)(2,1)}), bf16[16,2,16384]{2,1,0:T(2,128)(2,1)S(1)}, u32[]{:S(2)}, u32[]{:S(2)}) async-start(bf16[16,2,16384]{2,1,0:T(2,128)(2,1)} %reshape.164), calls=%async_computation | async-start | bytes 2097152 | tf_op jit(solution)/shard_map/all_to_all | solution.py:92
  72.9 4.2 %all-gather = s32[2,2,4]{2,1,0:T(2,128)S(1)} all-gather(s32[1,2,4]{2,1,0:T(2,128)S(1)} %bitcast.148), channel_id=1, replica_groups=mesh['dec'=2,'ada'=16] {'dec'}, dimensions={0}, use_global_device_ids=true | all-gather | bytes 96 | tf_op jit(solution)/shard_map/all_gather | solution.py:120
  77.2 0.7 dynamic-slice
  78.6 0.2 dynamic-update-slice
  78.8 4.3 %all-reduce = s32[4]{0:T(128)S(1)} all-reduce(s32[4]{0:T(128)S(1)} %dynamic-update-slice), channel_id=1, replica_groups=mesh['dec'=2,'ada'=16] {'dec'}, use_global_device_ids=true, to_apply=%add | all-reduce | flops 4 | bytes 32
  83.1 0.7 dynamic-slice.1
  84.9 1.7 gather_fusion
  86.8 0.9 copy.118
  87.8 12.3 %all-reduce.1 = s32[32]{0:T(128)S(1)} all-reduce(s32[32]{0:T(128)S(1)} %bitcast_dynamic-update-slice_fusion), channel_id=1, replica_groups=mesh['dec'=2,'ada'=16] {'ada'}, use_global_device_ids=true, to_apply=%add.1 | all-reduce | flops 32 | bytes 256 | tf_op jit(solution)/shard_map/squeeze | solution.py:74
  100.2 0.2 convert_reduce_fusion
  100.4 0.9 bitcast_bitcast_fusion
  101.3 7.0 %reshape.165 = bf16[8192,1,64]{2,1,0:T(2,128)(2,1)} reshape(bf16[16,2,16384]{2,1,0:T(2,128)(2,1)S(1)} %all-to-all-done) | data formatting | bytes 2097152
  108.3 2.5 %copy.115 = bf16[1,64,8192]{1,2,0:T(8,128)(2,1)S(1)} copy(bf16[1,64,8192]{1,0,2:T(2,128)(2,1)} %bitcast.123) | data formatting | bytes 2097152
  110.8 1.6 copy.80
  112.4 4.4 %fusion.19 = bf16[4,4,64]{2,1,0:T(4,128)(2,1)S(1)} fusion(bf16[4,32,8192]{2,0,1:T(4,128)(2,1)} %all-gather.3.cloned.1.call-done, bf16[1,8192,64]{1,2,0:T(8,128)(2,1)S(1)} %copy-done, s32[32]{0:T(128)S(1)} %get-tuple-element.11), kind=kOutput, calls=%fused_computation.24 | convolution fusion | flops 25298048 | bytes 3147904 | tf_op jit(solution)/shard_map/tjcd,jdr->tjcr/dot_general | solution.py:89
  116.8 19.0 %all_gather.22 = bf16[4,64,64]{2,0,1:T(4,128)(2,1)S(1)} all-gather(bf16[4,4,64]{2,0,1:T(4,128)(2,1)S(1)} %copy.76), channel_id=1, replica_groups=mesh['dec'=2,'ada'=16] {'ada'}, dimensions={1}, use_global_device_ids=true | all-gather | bytes 34816 | tf_op jit(solution)/shard_map/all_gather | solution.py:93
  135.8 1.5 fusion.7
  137.4 5.7 %fusion.1 = f32[4,32,512]{2,1,0:T(8,128)S(1)} fusion(bf16[8192,512]{1,0:T(8,128)(2,1)} %param.10, bf16[4,32,8192]{2,0,1:T(4,128)(2,1)S(1)} %copy-done.1), kind=kOutput, calls=%fused_computation.3 | convolution fusion | flops 1073741824 | bytes 10747904 | tf_op jit(solution)/shard_map/dot_general | solution.py:70
  143.2 0.2 fusion.15
  143.4 0.8 copy.84
  144.1 3.5 %all-to-all-start.1 = ((bf16[4,32,512]{2,0,1:T(4,128)(2,1)}), bf16[4,32,512]{2,0,1:T(4,128)(2,1)S(1)}, u32[]{:S(2)}, u32[]{:S(2)}) async-start(bf16[4,32,512]{2,0,1:T(4,128)(2,1)} %copy.84), calls=%async_computation.1 | async-start | bytes 262144 | tf_op jit(solution)/shard_map/all_to_all | solution.py:110
  147.7 1.1 bitcast_bitcast_fusion.1
  148.8 6.8 %all-to-all-done.1 = bf16[4,32,512]{2,0,1:T(4,128)(2,1)S(1)} async-done(((bf16[4,32,512]{2,0,1:T(4,128)(2,1)}), bf16[4,32,512]{2,0,1:T(4,128)(2,1)S(1)}, u32[]{:S(2)}, u32[]{:S(2)}) %all-to-all-start.1) | async-done | bytes 131104 | tf_op jit(solution)/shard_map/all_to_all | solution.py:110
  155.8 5.6 %all_gather.23 = bf16[4,4,8192]{2,0,1:T(4,128)(2,1)S(1)} all-gather(bf16[4,2,8192]{2,0,1:T(4,128)(2,1)S(1)} %all_to_all.42), channel_id=1, replica_groups=mesh['dec'=2,'ada'=16] {'dec'}, dimensions={1}, use_global_device_ids=true | all-gather | bytes 393216 | tf_op jit(solution)/shard_map/all_gather | solution.py:119
  161.4 0.3 reshape.161
  161.7 0.5 fusion.56
  162.2 0.4 fusion.27
  162.7 1.5 fusion.25
  164.1 0.7 reshape.166
  164.9 3.2 %all-to-all-start.3 = ((f32[2,1,512]{2,1,0:T(1,128)}), f32[2,1,512]{2,1,0:T(1,128)S(1)}, u32[]{:S(2)}, u32[]{:S(2)}) async-start(f32[2,1,512]{2,1,0:T(1,128)} %reshape.166), calls=%async_computation.3 | async-start | bytes 8192 | tf_op jit(solution)/shard_map/all_to_all | solution.py:136
  168.1 0.7 fusion.57
  169.0 0.7 reshape.168
  169.7 2.2 %all-to-all-done.3 = f32[2,1,512]{2,1,0:T(1,128)S(1)} async-done(((f32[2,1,512]{2,1,0:T(1,128)}), f32[2,1,512]{2,1,0:T(1,128)S(1)}, u32[]{:S(2)}, u32[]{:S(2)}) %all-to-all-start.3) | async-done | bytes 4128 | tf_op jit(solution)/shard_map/all_to_all | solution.py:136
  171.9 3.2 %all-to-all-start.4 = ((f32[2,1,512]{2,1,0:T(1,128)}), f32[2,1,512]{2,1,0:T(1,128)S(1)}, u32[]{:S(2)}, u32[]{:S(2)}) async-start(f32[2,1,512]{2,1,0:T(1,128)} %reshape.168), calls=%async_computation.4 | async-start | bytes 8192 | tf_op jit(solution)/shard_map/all_to_all | solution.py:137
  175.1 0.5 broadcast.161
  175.6 0.7 reduce.5
  176.4 2.4 %all-to-all-done.4 = f32[2,1,512]{2,1,0:T(1,128)S(1)} async-done(((f32[2,1,512]{2,1,0:T(1,128)}), f32[2,1,512]{2,1,0:T(1,128)S(1)}, u32[]{:S(2)}, u32[]{:S(2)}) %all-to-all-start.4) | async-done | bytes 4128 | tf_op jit(solution)/shard_map/all_to_all | solution.py:137
  178.9 3.5 %all-to-all-start.2 = ((f32[4,2,2,8,8,128]{5,4,0,3,2,1:T(8,128)}), f32[4,2,2,8,8,128]{5,4,0,3,2,1:T(8,128)S(1)}, u32[]{:S(2)}, u32[]{:S(2)}) async-start(f32[4,2,2,8,8,128]{5,4,0,3,2,1:T(8,128)} %bitcast.27), calls=%async_computation.2 | async-start | bytes 1048576 | tf_op jit(solution)/shard_map/all_to_all | solution.py:135
  182.4 0.7 reduce.6
  183.2 5.7 %all-to-all-done.2 = f32[4,2,2,8,8,128]{5,4,0,3,2,1:T(8,128)S(1)} async-done(((f32[4,2,2,8,8,128]{5,4,0,3,2,1:T(8,128)}), f32[4,2,2,8,8,128]{5,4,0,3,2,1:T(8,128)S(1)}, u32[]{:S(2)}, u32[]{:S(2)}) %all-to-all-start.2) | async-done | bytes 524320 | tf_op jit(solution)/shard_map/all_to_all | solution.py:135
  188.9 0.2 multiply_reduce_fusion
  189.1 0.5 fusion.16
  189.7 0.7 reshape.123
  (53 shorter events, 1.8 us)
Async XLA Ops:
  6.5 105.9 %copy-start = (bf16[1,8192,64]{1,2,0:T(8,128)(2,1)S(1)}, bf16[1,8192,64]{1,2,0:T(8,128)(2,1)}, u32[]{:S(2)}) copy-start(bf16[1,8192,64]{1,2,0:T(8,128)(2,1)} %param.11) | copy-start | bytes 3145732
  6.5 105.9 %all-gather.3.cloned.1.call-start = ((), (), s32[]{:S(2)}) async-start(), calls=%async_computation.5 | async-start | bytes 2228224 | tf_op jit(solution)/shard_map/all_gather | solution.py:67
  63.2 9.8 %copy-start.4 = (s32[2,4]{1,0:T(2,128)S(1)}, s32[2,4]{1,0:T(2,128)}, u32[]{:S(2)}) copy-start(s32[2,4]{1,0:T(2,128)} %param.16) | copy-start | bytes 100
  63.2 14.0 %copy-start.8 = (u32[32]{0:T(128)S(1)}, u32[32]{0:T(128)}, u32[]{:S(2)}) copy-start(u32[32]{0:T(128)} %constant.88) | copy-start | bytes 388
  63.2 15.4 %copy-start.5 = (s32[2]{0:T(128)S(1)}, s32[2]{0:T(128)}, u32[]{:S(2)}) copy-start(s32[2]{0:T(128)} %param.17) | copy-start | bytes 28
  63.2 19.9 %copy-start.7 = (u32[32]{0:T(128)S(1)}, u32[32]{0:T(128)}, u32[]{:S(2)}) copy-start(u32[32]{0:T(128)} %constant.93) | copy-start | bytes 388
  63.2 21.5 %copy-start.3 = (bf16[4,2,2,1024]{3,2,1,0:T(2,128)(2,1)S(1)}, bf16[4,2,2,1024]{3,2,1,0:T(2,128)(2,1)}, u32[]{:S(2)}) copy-start(bf16[4,2,2,1024]{3,2,1,0:T(2,128)(2,1)} %param.14) | copy-start | bytes 98308
  65.5 35.8 %all-to-all-start = ((bf16[16,2,16384]{2,1,0:T(2,128)(2,1)}), bf16[16,2,16384]{2,1,0:T(2,128)(2,1)S(1)}, u32[]{:S(2)}, u32[]{:S(2)}) async-start(bf16[16,2,16384]{2,1,0:T(2,128)(2,1)} %reshape.164), calls=%async_computation | async-start | bytes 2097152 | tf_op jit(solution)/shard_map/all_to_all | solution.py:92
  86.6 1.1 copy-start.6
  112.4 25.0 %copy-start.1 = (bf16[4,32,8192]{2,0,1:T(4,128)(2,1)S(1)}, bf16[4,32,8192]{2,0,1:T(4,128)(2,1)}, u32[]{:S(2)}) copy-start(bf16[4,32,8192]{2,0,1:T(4,128)(2,1)} %all-gather.3.cloned.1.call-done) | copy-start | bytes 6291460
  143.1 18.6 %copy-start.2 = (bf16[4,64,8,128,1]{3,2,1,0,4:T(8,128)(2,1)S(1)}, bf16[4,64,8,128,1]{3,2,1,0,4:T(8,128)(2,1)}, u32[]{:S(2)}) copy-start(bf16[4,64,8,128,1]{3,2,1,0,4:T(8,128)(2,1)} %bitcast_bitcast_fusion) | copy-start | bytes 1572868
  144.1 11.4 %all-to-all-start.1 = ((bf16[4,32,512]{2,0,1:T(4,128)(2,1)}), bf16[4,32,512]{2,0,1:T(4,128)(2,1)S(1)}, u32[]{:S(2)}, u32[]{:S(2)}) async-start(bf16[4,32,512]{2,0,1:T(4,128)(2,1)} %copy.84), calls=%async_computation.1 | async-start | bytes 262144 | tf_op jit(solution)/shard_map/all_to_all | solution.py:110
  164.9 7.0 %all-to-all-start.3 = ((f32[2,1,512]{2,1,0:T(1,128)}), f32[2,1,512]{2,1,0:T(1,128)S(1)}, u32[]{:S(2)}, u32[]{:S(2)}) async-start(f32[2,1,512]{2,1,0:T(1,128)} %reshape.166), calls=%async_computation.3 | async-start | bytes 8192 | tf_op jit(solution)/shard_map/all_to_all | solution.py:136
  171.9 7.0 %all-to-all-start.4 = ((f32[2,1,512]{2,1,0:T(1,128)}), f32[2,1,512]{2,1,0:T(1,128)S(1)}, u32[]{:S(2)}, u32[]{:S(2)}) async-start(f32[2,1,512]{2,1,0:T(1,128)} %reshape.168), calls=%async_computation.4 | async-start | bytes 8192 | tf_op jit(solution)/shard_map/all_to_all | solution.py:137
  178.9 10.1 %all-to-all-start.2 = ((f32[4,2,2,8,8,128]{5,4,0,3,2,1:T(8,128)}), f32[4,2,2,8,8,128]{5,4,0,3,2,1:T(8,128)S(1)}, u32[]{:S(2)}, u32[]{:S(2)}) async-start(f32[4,2,2,8,8,128]{5,4,0,3,2,1:T(8,128)} %bitcast.27), calls=%async_computation.2 | async-start | bytes 1048576 | tf_op jit(solution)/shard_map/all_to_all | solution.py:135
Sparse Core Ops, SparseCore 0:
  9.5 44.1 all-gather.2
where the time goes:
time: 198 us; the launch traced here: 197 us
  other arithmetic  47.7 us (24%)
  blocking collectives  45.5 us (23%)
  local copies, waits for them, and re-layouts  36 us (18%)
  starting transfers between devices  20.9 us (11%)
  waiting for transfers between devices  17.1 us (9%)
  between operations  15.1 us (8%)
  matrix products  15 us (8%)
    unnamed x1, other arithmetic  45.2 us
    unnamed x36, local copies, waits for them, and re-layouts  27.6 us
    all_gather x1, blocking collectives, body(): lax.all_gather(shrink.reshape(steps, slots, adapter_rank), 'ada', axis=1,...  19 us
    squeeze x1, blocking collectives, body(): row_adapter = group_ids[:, 0]  12.3 us
    all_to_all x1, starting transfers between devices, body(): lax.all_to_all(adapter_up, 'ada', split_axis=2, concat_axis=0, tiled=True)  7.42 us
    all_to_all x1, waiting for transfers between devices, body(): lax.all_to_all(query_columns, 'ada', split_axis=1, concat_axis=2, tiled=T...  6.79 us
    dot_general x1, matrix products, body(): jnp.dot(whole_inputs.reshape(steps * group, width), query_weight, preferr...  5.7 us
    all_to_all x1, waiting for transfers between devices, body(): lax.all_to_all(partial_numerator, 'dec', split_axis=1, concat_axis=1, til...  5.68 us
  transfers between devices with their start and end apart: 6, of which 4 were waited for; matrix products, arithmetic and copies ran while one was open for 40% of the time, Pallas kernels for 0%

commit v1 on v0

--- a/solution.py
+++ b/solution.py
@@ -10,6 +10,18 @@
 CAP = 4
 NEGATIVE = -1e30
 HIGH = lax.Precision.HIGHEST
+
+
+def in_blocks(array, dim, devices):
+    lengths = array.shape
+    blocks = array.reshape(*lengths[:dim], devices, lengths[dim] // devices, *lengths[dim + 1 :])
+    return jnp.moveaxis(blocks, dim, 0)
+
+
+def in_order(parts, dim):
+    parts = jnp.moveaxis(parts, 0, dim)
+    shape = parts.shape
+    return parts.reshape(*shape[:dim], shape[dim] * shape[dim + 1], *shape[dim + 2 :])
 
 
 def cache_part(query, keys, values, live):
@@ -107,7 +119,14 @@
         "mr,urx->umx", slot_position, received_rows, preferred_element_type=jnp.float32
     )
     query_columns = (base_output + low_rank_update).astype(jnp.bfloat16)
-    query_local = lax.all_to_all(query_columns, "ada", split_axis=1, concat_axis=2, tiled=True)
+    peers, index = (lax.axis_size("ada"), lax.axis_index("ada"))
+    blocks = in_blocks(query_columns, 1, peers)
+    done = [blocks[index]]
+    for step in range(1, peers):
+        sent = blocks[index ^ step]
+        done.append(lax.ppermute(sent, "ada", [(i, i ^ step) for i in range(peers)]))
+    blocks = jnp.stack(done)[index ^ jnp.arange(peers)]
+    query_local = in_order(blocks, 2)
     group_heads = HEADS // KVH
     query = query_local.reshape(steps, row_local, KVH, group_heads, HD)
     fresh = fresh_part(query, new_cache)

time: 198 us -> 214 us (1.081)
  starting transfers between devices: 20.9 us -> 38.4 us
  waiting for transfers between devices: 17.1 us -> 12.3 us
  blocking collectives: 45.5 us -> 48.2 us
    ppermute x0 -> x15, starting transfers between devices: none -> 21.1 us  [body(): lax.ppermute(sent, 'ada', [(i, i ^ step) for i in range(peers)])]
    all_to_all x1 -> x0, waiting for transfers between devices: 6.79 us -> none  [body(): lax.all_to_all(query_columns, 'ada', split_axis=1, concat_axis=2, tiled=T...]
    all_to_all x1 -> x0, starting transfers between devices: 3.51 us -> none  [body(): lax.all_to_all(query_columns, 'ada', split_axis=1, concat_axis=2, tiled=T...]
    unnamed x36 -> x53, local copies, waits for them, and re-layouts: 27.6 us -> 27.2 us
  transfers between devices with their start and end apart: 6 -> 20, of which waited for: 4 -> 4; matrix products, arithmetic and copies ran while one was open for 40% -> 37% of each run, Pallas kernels for 0% -> 0%
where the time goes in v1:
time: 214 us; the launch traced here: 213 us
  blocking collectives  48.2 us (23%)
  other arithmetic  47.7 us (22%)
  starting transfers between devices  38.4 us (18%)
  local copies, waits for them, and re-layouts  35.5 us (17%)
  between operations  15.5 us (7%)
  matrix products  15 us (7%)
  waiting for transfers between devices  12.3 us (6%)
    unnamed x1, other arithmetic  45.2 us
    unnamed x53, local copies, waits for them, and re-layouts  27.2 us
    ppermute x15, starting transfers between devices, body(): lax.ppermute(sent, 'ada', [(i, i ^ step) for i in range(peers)])  21.1 us
    all_gather x1, blocking collectives, body(): lax.all_gather(shrink.reshape(steps, slots, adapter_rank), 'ada', axis=1,...  19.6 us
    squeeze x1, blocking collectives, body(): row_adapter = group_ids[:, 0]  13.9 us
    all_to_all x1, starting transfers between devices, body(): lax.all_to_all(adapter_up, 'ada', split_axis=2, concat_axis=0, tiled=True)  7.42 us
    all_gather x1, blocking collectives, body(): lax.all_gather(query_local, 'dec', axis=1, tiled=True)  6.16 us
    dot_general x1, matrix products, body(): jnp.dot(whole_inputs.reshape(steps * group, width), query_weight, preferr...  5.69 us
  transfers between devices with their start and end apart: 20, of which 4 were waited for; matrix products, arithmetic and copies ran while one was open for 37% of the time, Pallas kernels for 0%

profile of v1, /device:TPU:0, one launch (start us, length us, event | category | flops | bytes accessed | tf_op | source)
XLA Modules:
  0.0 212.5 jit_solution(9076290997978294312)
XLA Ops:
  6.5 1.8 copy.135
  8.3 9.2 %copy.140 = bf16[1,64,8192]{1,0,2:T(2,128)(2,1)} copy(bf16[1,64,8192]{2,1,0:T(8,128)(2,1)} %param.12) | data formatting | bytes 2097152 | tf_op args[3]
  17.5 0.5 broadcast.195
  18.0 45.2 %reduce.4 = bf16[8192,64]{1,0:T(8,128)(2,1)S(1)} reduce(bf16[8192,1,64]{2,1,0:T(2,128)(2,1)} %bitcast.193, bf16[]{:T(256)} %broadcast.195), dimensions={1}, to_apply=%bitcast.161.reduce_sub_computation | reduce | bytes 2097154
  63.2 2.3 %reshape.223 = bf16[16,2,16384]{2,1,0:T(2,128)(2,1)} reshape(bf16[8192,64]{1,0:T(8,128)(2,1)S(1)} %reduce.4) | data formatting | bytes 2097152
  65.5 0.7 dynamic-slice.64
  67.1 7.4 %all-to-all-start = ((bf16[16,2,16384]{2,1,0:T(2,128)(2,1)}), bf16[16,2,16384]{2,1,0:T(2,128)(2,1)S(1)}, u32[]{:S(2)}, u32[]{:S(2)}) async-start(bf16[16,2,16384]{2,1,0:T(2,128)(2,1)} %reshape.223), calls=%async_computation | async-start | bytes 2097152 | tf_op jit(solution)/shard_map/all_to_all | solution.py:104
  74.5 4.3 %all-reduce = s32[4]{0:T(128)S(1)} all-reduce(s32[4]{0:T(128)S(1)} %dynamic-update-slice), channel_id=1, replica_groups=mesh['dec'=2,'ada'=16] {'dec'}, use_global_device_ids=true, to_apply=%add | all-reduce | flops 4 | bytes 32
  78.8 4.2 %all-gather = s32[2,2,4]{2,1,0:T(2,128)S(1)} all-gather(s32[1,2,4]{2,1,0:T(2,128)S(1)} %bitcast.233), channel_id=1, replica_groups=mesh['dec'=2,'ada'=16] {'dec'}, dimensions={0}, use_global_device_ids=true | all-gather | bytes 96 | tf_op jit(solution)/shard_map/all_gather | solution.py:139
  83.1 0.7 dynamic-slice.65
  84.9 1.7 gather_fusion
  87.3 13.9 %all-reduce.1 = s32[32]{0:T(128)S(1)} all-reduce(s32[32]{0:T(128)S(1)} %bitcast_dynamic-update-slice_fusion), channel_id=1, replica_groups=mesh['dec'=2,'ada'=16] {'ada'}, use_global_device_ids=true, to_apply=%add.1 | all-reduce | flops 32 | bytes 256 | tf_op jit(solution)/shard_map/squeeze | solution.py:86
  101.5 0.9 bitcast_bitcast_fusion
  102.4 0.8 bitcast_bitcast_fusion.1
  103.2 7.0 %reshape.224 = bf16[8192,1,64]{2,1,0:T(2,128)(2,1)} reshape(bf16[16,2,16384]{2,1,0:T(2,128)(2,1)S(1)} %all-to-all-done) | data formatting | bytes 2097152
  110.2 2.5 %copy.194 = bf16[1,64,8192]{1,2,0:T(8,128)(2,1)S(1)} copy(bf16[1,64,8192]{1,0,2:T(2,128)(2,1)} %bitcast.194) | data formatting | bytes 2097152
  112.7 1.6 copy.142
  114.4 4.4 %fusion.19 = bf16[4,4,64]{2,1,0:T(4,128)(2,1)S(1)} fusion(bf16[4,32,8192]{2,0,1:T(4,128)(2,1)} %all-gather.3.cloned.1.call-done, bf16[1,8192,64]{1,2,0:T(8,128)(2,1)S(1)} %copy-done, s32[32]{0:T(128)S(1)} %get-tuple-element.11), kind=kOutput, calls=%fused_computation.25 | convolution fusion | flops 25298048 | bytes 3147904 | tf_op jit(solution)/shard_map/tjcd,jdr->tjcr/dot_general | solution.py:101
  118.7 19.6 %all_gather.22 = bf16[4,64,64]{2,0,1:T(4,128)(2,1)S(1)} all-gather(bf16[4,4,64]{2,0,1:T(4,128)(2,1)S(1)} %copy.138), channel_id=1, replica_groups=mesh['dec'=2,'ada'=16] {'ada'}, dimensions={1}, use_global_device_ids=true | all-gather | bytes 34816 | tf_op jit(solution)/shard_map/all_gather | solution.py:105
  138.4 1.5 fusion.7
  140.0 5.7 %fusion.1 = f32[4,32,512]{2,1,0:T(8,128)S(1)} fusion(bf16[8192,512]{1,0:T(8,128)(2,1)} %param.10, bf16[4,32,8192]{2,0,1:T(4,128)(2,1)S(1)} %copy-done.1), kind=kOutput, calls=%fused_computation.4 | convolution fusion | flops 1073741824 | bytes 10747904 | tf_op jit(solution)/shard_map/dot_general | solution.py:82
  146.6 1.5 collective-permute-start.2
  148.1 2.0 collective-permute-start.4
  150.4 2.4 %collective-permute-start.6 = (bf16[4,2,512]{2,0,1:T(4,128)(2,1)S(1)}, bf16[4,2,512]{2,0,1:T(4,128)(2,1)S(1)}, u32[]{:S(2)}, u32[]{:S(2)}) collective-permute-start(bf16[4,2,512]{2,0,1:T(4,128)(2,1)S(1)} %bitcast.229), channel_id=1, source_target_pairs={{0,7},{1,6},{2,5},{3,4},{4,3},{5,2},{6,1},{7,0},{8,15},{9,14},{10,... | collective-permute-start | bytes 24584 | tf_op jit(solution)/shard_map/ppermute | solution.py:127
  152.9 2.9 %collective-permute-start.8 = (bf16[4,2,512]{2,0,1:T(4,128)(2,1)S(1)}, bf16[4,2,512]{2,0,1:T(4,128)(2,1)S(1)}, u32[]{:S(2)}, u32[]{:S(2)}) collective-permute-start(bf16[4,2,512]{2,0,1:T(4,128)(2,1)S(1)} %bitcast.225), channel_id=1, source_target_pairs={{0,9},{1,8},{2,11},{3,10},{4,13},{5,12},{6,15},{7,14},{8,1},{9,0},... | collective-permute-start | bytes 24584 | tf_op jit(solution)/shard_map/ppermute | solution.py:127
  156.0 3.3 %collective-permute-start.10 = (bf16[4,2,512]{2,0,1:T(4,128)(2,1)S(1)}, bf16[4,2,512]{2,0,1:T(4,128)(2,1)S(1)}, u32[]{:S(2)}, u32[]{:S(2)}) collective-permute-start(bf16[4,2,512]{2,0,1:T(4,128)(2,1)S(1)} %bitcast.222), channel_id=1, source_target_pairs={{0,11},{1,10},{2,9},{3,8},{4,15},{5,14},{6,13},{7,12},{8,3},{9,2},... | collective-permute-start | bytes 24584 | tf_op jit(solution)/shard_map/ppermute | solution.py:127
  159.4 3.8 %collective-permute-start.12 = (bf16[4,2,512]{2,0,1:T(4,128)(2,1)S(1)}, bf16[4,2,512]{2,0,1:T(4,128)(2,1)S(1)}, u32[]{:S(2)}, u32[]{:S(2)}) collective-permute-start(bf16[4,2,512]{2,0,1:T(4,128)(2,1)S(1)} %bitcast.220), channel_id=1, source_target_pairs={{0,13},{1,12},{2,15},{3,14},{4,9},{5,8},{6,11},{7,10},{8,5},{9,4},... | collective-permute-start | bytes 24584 | tf_op jit(solution)/shard_map/ppermute | solution.py:127
  163.4 4.2 %collective-permute-start.14 = (bf16[4,2,512]{2,0,1:T(4,128)(2,1)S(1)}, bf16[4,2,512]{2,0,1:T(4,128)(2,1)S(1)}, u32[]{:S(2)}, u32[]{:S(2)}) collective-permute-start(bf16[4,2,512]{2,0,1:T(4,128)(2,1)S(1)} %bitcast.218), channel_id=1, source_target_pairs={{0,15},{1,14},{2,13},{3,12},{4,11},{5,10},{6,9},{7,8},{8,7},{9,6},... | collective-permute-start | bytes 24584 | tf_op jit(solution)/shard_map/ppermute | solution.py:127
  167.7 2.0 collective-permute-done.13
  169.7 0.7 gather_fusion.1
  170.6 6.2 %all_gather.23 = bf16[4,4,8192]{2,0,1:T(4,128)(2,1)S(1)} all-gather(bf16[4,2,8192]{2,0,1:T(4,128)(2,1)S(1)} %bitcast.204), channel_id=1, replica_groups=mesh['dec'=2,'ada'=16] {'dec'}, dimensions={1}, use_global_device_ids=true | all-gather | bytes 393216 | tf_op jit(solution)/shard_map/all_gather | solution.py:138
  177.0 0.5 fusion.57
  177.5 0.4 fusion.27
  178.0 1.5 fusion.25
  179.4 0.7 reshape.225
  180.2 3.2 %all-to-all-start.2 = ((f32[2,1,512]{2,1,0:T(1,128)}), f32[2,1,512]{2,1,0:T(1,128)S(1)}, u32[]{:S(2)}, u32[]{:S(2)}) async-start(f32[2,1,512]{2,1,0:T(1,128)} %reshape.225), calls=%async_computation.2 | async-start | bytes 8192 | tf_op jit(solution)/shard_map/all_to_all | solution.py:155
  183.4 0.7 fusion.58
  184.3 0.7 reshape.227
  185.0 2.2 %all-to-all-done.2 = f32[2,1,512]{2,1,0:T(1,128)S(1)} async-done(((f32[2,1,512]{2,1,0:T(1,128)}), f32[2,1,512]{2,1,0:T(1,128)S(1)}, u32[]{:S(2)}, u32[]{:S(2)}) %all-to-all-start.2) | async-done | bytes 4128 | tf_op jit(solution)/shard_map/all_to_all | solution.py:155
  187.2 3.2 %all-to-all-start.3 = ((f32[2,1,512]{2,1,0:T(1,128)}), f32[2,1,512]{2,1,0:T(1,128)S(1)}, u32[]{:S(2)}, u32[]{:S(2)}) async-start(f32[2,1,512]{2,1,0:T(1,128)} %reshape.227), calls=%async_computation.3 | async-start | bytes 8192 | tf_op jit(solution)/shard_map/all_to_all | solution.py:156
  190.4 0.5 broadcast.196
  190.9 0.7 reduce.5
  191.8 2.4 %all-to-all-done.3 = f32[2,1,512]{2,1,0:T(1,128)S(1)} async-done(((f32[2,1,512]{2,1,0:T(1,128)}), f32[2,1,512]{2,1,0:T(1,128)S(1)}, u32[]{:S(2)}, u32[]{:S(2)}) %all-to-all-start.3) | async-done | bytes 4128 | tf_op jit(solution)/shard_map/all_to_all | solution.py:156
  194.2 3.5 %all-to-all-start.1 = ((f32[4,2,2,8,8,128]{5,4,0,3,2,1:T(8,128)}), f32[4,2,2,8,8,128]{5,4,0,3,2,1:T(8,128)S(1)}, u32[]{:S(2)}, u32[]{:S(2)}) async-start(f32[4,2,2,8,8,128]{5,4,0,3,2,1:T(8,128)} %bitcast.57), calls=%async_computation.1 | async-start | bytes 1048576 | tf_op jit(solution)/shard_map/all_to_all | solution.py:154
  197.7 0.7 reduce.6
  198.5 5.7 %all-to-all-done.1 = f32[4,2,2,8,8,128]{5,4,0,3,2,1:T(8,128)S(1)} async-done(((f32[4,2,2,8,8,128]{5,4,0,3,2,1:T(8,128)}), f32[4,2,2,8,8,128]{5,4,0,3,2,1:T(8,128)S(1)}, u32[]{:S(2)}, u32[]{:S(2)}) %all-to-all-start.1) | async-done | bytes 524320 | tf_op jit(solution)/shard_map/all_to_all | solution.py:154
  204.4 0.5 fusion.16
  205.0 0.7 reshape.173
  (117 shorter events, 4.6 us)
Async XLA Ops:
  6.5 107.8 %copy-start = (bf16[1,8192,64]{1,2,0:T(8,128)(2,1)S(1)}, bf16[1,8192,64]{1,2,0:T(8,128)(2,1)}, u32[]{:S(2)}) copy-start(bf16[1,8192,64]{1,2,0:T(8,128)(2,1)} %param.11) | copy-start | bytes 3145732
  6.5 107.8 %all-gather.3.cloned.1.call-start = ((), (), s32[]{:S(2)}) async-start(), calls=%async_computation.4 | async-start | bytes 2228224 | tf_op jit(solution)/shard_map/all_gather | solution.py:79
  63.2 2.3 %copy-start.9 = (u32[32]{0:T(128)S(1)}, u32[32]{0:T(128)}, u32[]{:S(2)}) copy-start(u32[32]{0:T(128)} %constant.114) | copy-start | bytes 388
  63.2 3.7 %copy-start.6 = (s32[2]{0:T(128)S(1)}, s32[2]{0:T(128)}, u32[]{:S(2)}) copy-start(s32[2]{0:T(128)} %param.17) | copy-start | bytes 28
  63.2 15.6 %copy-start.5 = (s32[2,4]{1,0:T(2,128)S(1)}, s32[2,4]{1,0:T(2,128)}, u32[]{:S(2)}) copy-start(s32[2,4]{1,0:T(2,128)} %param.16) | copy-start | bytes 100
  63.2 19.9 %copy-start.8 = (u32[32]{0:T(128)S(1)}, u32[32]{0:T(128)}, u32[]{:S(2)}) copy-start(u32[32]{0:T(128)} %constant.119) | copy-start | bytes 388
  63.2 21.5 %copy-start.4 = (bf16[4,2,2,1024]{3,2,1,0:T(2,128)(2,1)S(1)}, bf16[4,2,2,1024]{3,2,1,0:T(2,128)(2,1)}, u32[]{:S(2)}) copy-start(bf16[4,2,2,1024]{3,2,1,0:T(2,128)(2,1)} %param.14) | copy-start | bytes 98308
  67.1 36.1 %all-to-all-start = ((bf16[16,2,16384]{2,1,0:T(2,128)(2,1)}), bf16[16,2,16384]{2,1,0:T(2,128)(2,1)S(1)}, u32[]{:S(2)}, u32[]{:S(2)}) async-start(bf16[16,2,16384]{2,1,0:T(2,128)(2,1)} %reshape.223), calls=%async_computation | async-start | bytes 2097152 | tf_op jit(solution)/shard_map/all_to_all | solution.py:104
  86.6 0.7 copy-start.7
  114.3 25.6 %copy-start.1 = (bf16[4,32,8192]{2,0,1:T(4,128)(2,1)S(1)}, bf16[4,32,8192]{2,0,1:T(4,128)(2,1)}, u32[]{:S(2)}) copy-start(bf16[4,32,8192]{2,0,1:T(4,128)(2,1)} %all-gather.3.cloned.1.call-done) | copy-start | bytes 6291460
  145.7 31.4 %copy-start.3 = (bf16[4,64,8,128,1]{3,2,1,0,4:T(8,128)(2,1)S(1)}, bf16[4,64,8,128,1]{3,2,1,0,4:T(8,128)(2,1)}, u32[]{:S(2)}) copy-start(bf16[4,64,8,128,1]{3,2,1,0,4:T(8,128)(2,1)} %bitcast_bitcast_fusion) | copy-start | bytes 1572868
  146.2 4.0 %collective-permute-start = (bf16[4,2,512]{2,0,1:T(4,128)(2,1)S(1)}, bf16[4,2,512]{2,0,1:T(4,128)(2,1)S(1)}, u32[]{:S(2)}, u32[]{:S(2)}) collective-permute-start(bf16[4,2,512]{2,0,1:T(4,128)(2,1)S(1)} %bitcast.232), channel_id=1, source_target_pairs={{0,1},{1,0},{2,3},{3,2},{4,5},{5,4},{6,7},{7,6},{8,9},{9,8},{10,11... | collective-permute-start | bytes 24584 | tf_op jit(solution)/shard_map/ppermute | solution.py:127
  146.6 3.7 %collective-permute-start.1 = (bf16[4,2,512]{2,0,1:T(4,128)(2,1)S(1)}, bf16[4,2,512]{2,0,1:T(4,128)(2,1)S(1)}, u32[]{:S(2)}, u32[]{:S(2)}) collective-permute-start(bf16[4,2,512]{2,0,1:T(4,128)(2,1)S(1)} %bitcast.230), channel_id=1, source_target_pairs={{0,2},{1,3},{2,0},{3,1},{4,6},{5,7},{6,4},{7,5},{8,10},{9,11},{10,... | collective-permute-start | bytes 24584 | tf_op jit(solution)/shard_map/ppermute | solution.py:127
  146.6 6.2 %collective-permute-start.2 = (bf16[4,2,512]{2,0,1:T(4,128)(2,1)S(1)}, bf16[4,2,512]{2,0,1:T(4,128)(2,1)S(1)}, u32[]{:S(2)}, u32[]{:S(2)}) collective-permute-start(bf16[4,2,512]{2,0,1:T(4,128)(2,1)S(1)} %bitcast.228), channel_id=1, source_target_pairs={{0,3},{1,2},{2,1},{3,0},{4,7},{5,6},{6,5},{7,4},{8,11},{9,10},{10,... | collective-permute-start | bytes 24584 | tf_op jit(solution)/shard_map/ppermute | solution.py:127
  148.1 4.8 %collective-permute-start.3 = (bf16[4,2,512]{2,0,1:T(4,128)(2,1)S(1)}, bf16[4,2,512]{2,0,1:T(4,128)(2,1)S(1)}, u32[]{:S(2)}, u32[]{:S(2)}) collective-permute-start(bf16[4,2,512]{2,0,1:T(4,128)(2,1)S(1)} %bitcast.226), channel_id=1, source_target_pairs={{0,4},{1,5},{2,6},{3,7},{4,0},{5,1},{6,2},{7,3},{8,12},{9,13},{10,... | collective-permute-start | bytes 24584 | tf_op jit(solution)/shard_map/ppermute | solution.py:127
  148.1 7.7 %collective-permute-start.4 = (bf16[4,2,512]{2,0,1:T(4,128)(2,1)S(1)}, bf16[4,2,512]{2,0,1:T(4,128)(2,1)S(1)}, u32[]{:S(2)}, u32[]{:S(2)}) collective-permute-start(bf16[4,2,512]{2,0,1:T(4,128)(2,1)S(1)} %bitcast.224), channel_id=1, source_target_pairs={{0,5},{1,4},{2,7},{3,6},{4,1},{5,0},{6,3},{7,2},{8,13},{9,12},{10,... | collective-permute-start | bytes 24584 | tf_op jit(solution)/shard_map/ppermute | solution.py:127
  150.3 5.7 %collective-permute-start.5 = (bf16[4,2,512]{2,0,1:T(4,128)(2,1)S(1)}, bf16[4,2,512]{2,0,1:T(4,128)(2,1)S(1)}, u32[]{:S(2)}, u32[]{:S(2)}) collective-permute-start(bf16[4,2,512]{2,0,1:T(4,128)(2,1)S(1)} %bitcast.231), channel_id=1, source_target_pairs={{0,6},{1,7},{2,4},{3,5},{4,2},{5,3},{6,0},{7,1},{8,14},{9,15},{10,... | collective-permute-start | bytes 24584 | tf_op jit(solution)/shard_map/ppermute | solution.py:127
  150.4 9.0 %collective-permute-start.6 = (bf16[4,2,512]{2,0,1:T(4,128)(2,1)S(1)}, bf16[4,2,512]{2,0,1:T(4,128)(2,1)S(1)}, u32[]{:S(2)}, u32[]{:S(2)}) collective-permute-start(bf16[4,2,512]{2,0,1:T(4,128)(2,1)S(1)} %bitcast.229), channel_id=1, source_target_pairs={{0,7},{1,6},{2,5},{3,4},{4,3},{5,2},{6,1},{7,0},{8,15},{9,14},{10,... | collective-permute-start | bytes 24584 | tf_op jit(solution)/shard_map/ppermute | solution.py:127
  152.8 6.6 %collective-permute-start.7 = (bf16[4,2,512]{2,0,1:T(4,128)(2,1)S(1)}, bf16[4,2,512]{2,0,1:T(4,128)(2,1)S(1)}, u32[]{:S(2)}, u32[]{:S(2)}) collective-permute-start(bf16[4,2,512]{2,0,1:T(4,128)(2,1)S(1)} %bitcast.227), channel_id=1, source_target_pairs={{0,8},{1,9},{2,10},{3,11},{4,12},{5,13},{6,14},{7,15},{8,0},{9,1},... | collective-permute-start | bytes 24584 | tf_op jit(solution)/shard_map/ppermute | solution.py:127
  152.9 10.3 %collective-permute-start.8 = (bf16[4,2,512]{2,0,1:T(4,128)(2,1)S(1)}, bf16[4,2,512]{2,0,1:T(4,128)(2,1)S(1)}, u32[]{:S(2)}, u32[]{:S(2)}) collective-permute-start(bf16[4,2,512]{2,0,1:T(4,128)(2,1)S(1)} %bitcast.225), channel_id=1, source_target_pairs={{0,9},{1,8},{2,11},{3,10},{4,13},{5,12},{6,15},{7,14},{8,1},{9,0},... | collective-permute-start | bytes 24584 | tf_op jit(solution)/shard_map/ppermute | solution.py:127
  155.9 7.5 %collective-permute-start.9 = (bf16[4,2,512]{2,0,1:T(4,128)(2,1)S(1)}, bf16[4,2,512]{2,0,1:T(4,128)(2,1)S(1)}, u32[]{:S(2)}, u32[]{:S(2)}) collective-permute-start(bf16[4,2,512]{2,0,1:T(4,128)(2,1)S(1)} %bitcast.223), channel_id=1, source_target_pairs={{0,10},{1,11},{2,8},{3,9},{4,14},{5,15},{6,12},{7,13},{8,2},{9,3},... | collective-permute-start | bytes 24584 | tf_op jit(solution)/shard_map/ppermute | solution.py:127
  156.0 11.7 %collective-permute-start.10 = (bf16[4,2,512]{2,0,1:T(4,128)(2,1)S(1)}, bf16[4,2,512]{2,0,1:T(4,128)(2,1)S(1)}, u32[]{:S(2)}, u32[]{:S(2)}) collective-permute-start(bf16[4,2,512]{2,0,1:T(4,128)(2,1)S(1)} %bitcast.222), channel_id=1, source_target_pairs={{0,11},{1,10},{2,9},{3,8},{4,15},{5,14},{6,13},{7,12},{8,3},{9,2},... | collective-permute-start | bytes 24584 | tf_op jit(solution)/shard_map/ppermute | solution.py:127
  159.3 8.3 %collective-permute-start.11 = (bf16[4,2,512]{2,0,1:T(4,128)(2,1)S(1)}, bf16[4,2,512]{2,0,1:T(4,128)(2,1)S(1)}, u32[]{:S(2)}, u32[]{:S(2)}) collective-permute-start(bf16[4,2,512]{2,0,1:T(4,128)(2,1)S(1)} %bitcast.221), channel_id=1, source_target_pairs={{0,12},{1,13},{2,14},{3,15},{4,8},{5,9},{6,10},{7,11},{8,4},{9,5},... | collective-permute-start | bytes 24584 | tf_op jit(solution)/shard_map/ppermute | solution.py:127
  159.4 8.2 %collective-permute-start.12 = (bf16[4,2,512]{2,0,1:T(4,128)(2,1)S(1)}, bf16[4,2,512]{2,0,1:T(4,128)(2,1)S(1)}, u32[]{:S(2)}, u32[]{:S(2)}) collective-permute-start(bf16[4,2,512]{2,0,1:T(4,128)(2,1)S(1)} %bitcast.220), channel_id=1, source_target_pairs={{0,13},{1,12},{2,15},{3,14},{4,9},{5,8},{6,11},{7,10},{8,5},{9,4},... | collective-permute-start | bytes 24584 | tf_op jit(solution)/shard_map/ppermute | solution.py:127
  163.3 6.4 %collective-permute-start.13 = (bf16[4,2,512]{2,0,1:T(4,128)(2,1)S(1)}, bf16[4,2,512]{2,0,1:T(4,128)(2,1)S(1)}, u32[]{:S(2)}, u32[]{:S(2)}) collective-permute-start(bf16[4,2,512]{2,0,1:T(4,128)(2,1)S(1)} %bitcast.219), channel_id=1, source_target_pairs={{0,14},{1,15},{2,12},{3,13},{4,10},{5,11},{6,8},{7,9},{8,6},{9,7},... | collective-permute-start | bytes 24584 | tf_op jit(solution)/shard_map/ppermute | solution.py:127
  163.4 6.3 %collective-permute-start.14 = (bf16[4,2,512]{2,0,1:T(4,128)(2,1)S(1)}, bf16[4,2,512]{2,0,1:T(4,128)(2,1)S(1)}, u32[]{:S(2)}, u32[]{:S(2)}) collective-permute-start(bf16[4,2,512]{2,0,1:T(4,128)(2,1)S(1)} %bitcast.218), channel_id=1, source_target_pairs={{0,15},{1,14},{2,13},{3,12},{4,11},{5,10},{6,9},{7,8},{8,7},{9,6},... | collective-permute-start | bytes 24584 | tf_op jit(solution)/shard_map/ppermute | solution.py:127
  167.6 10.3 %copy-start.2 = (bf16[4,64,8,128,1]{3,2,1,0,4:T(8,128)(2,1)S(1)}, bf16[4,64,8,128,1]{3,2,1,0,4:T(8,128)(2,1)}, u32[]{:S(2)}) copy-start(bf16[4,64,8,128,1]{3,2,1,0,4:T(8,128)(2,1)} %bitcast_bitcast_fusion.1) | copy-start | bytes 1572868
  180.2 7.0 %all-to-all-start.2 = ((f32[2,1,512]{2,1,0:T(1,128)}), f32[2,1,512]{2,1,0:T(1,128)S(1)}, u32[]{:S(2)}, u32[]{:S(2)}) async-start(f32[2,1,512]{2,1,0:T(1,128)} %reshape.225), calls=%async_computation.2 | async-start | bytes 8192 | tf_op jit(solution)/shard_map/all_to_all | solution.py:155
  187.2 7.0 %all-to-all-start.3 = ((f32[2,1,512]{2,1,0:T(1,128)}), f32[2,1,512]{2,1,0:T(1,128)S(1)}, u32[]{:S(2)}, u32[]{:S(2)}) async-start(f32[2,1,512]{2,1,0:T(1,128)} %reshape.227), calls=%async_computation.3 | async-start | bytes 8192 | tf_op jit(solution)/shard_map/all_to_all | solution.py:156
  194.2 10.1 %all-to-all-start.1 = ((f32[4,2,2,8,8,128]{5,4,0,3,2,1:T(8,128)}), f32[4,2,2,8,8,128]{5,4,0,3,2,1:T(8,128)S(1)}, u32[]{:S(2)}, u32[]{:S(2)}) async-start(f32[4,2,2,8,8,128]{5,4,0,3,2,1:T(8,128)} %bitcast.57), calls=%async_computation.1 | async-start | bytes 1048576 | tf_op jit(solution)/shard_map/all_to_all | solution.py:154
Sparse Core Ops, SparseCore 0:
  9.5 44.1 all-gather.2
